TPU v7x, 32 devices: a whole 2x2x4 slice. The times are simulated.
32 devices in a mesh: rep: 8 (over z, x), shard: 4 (over y, core).
Axes of the slice: x: 2, y: 2, z: 4, core: 2. Of those that a mesh axis runs over, the one named last changes fastest.
Arguments:
- latent_tokens: bfloat16 [256, 256, 384], P(('rep', 'shard')), may hold values from -6 to 6
- cond: bfloat16 [256, 384], P(('rep', 'shard')), may hold values from -6 to 6
- w_ada: bfloat16 [384, 2304], P('shard'), may hold values from -0.3125 to 0.3125
- b_ada: bfloat16 [2304], P('shard'), may hold values from -3 to 3
- w_qkv: bfloat16 [384, 1152], P('shard'), may hold values from -0.3125 to 0.3125
- b_qv: bfloat16 [768], P('shard'), may hold values from -3 to 3
- w_o: bfloat16 [384, 384], P('shard'), may hold values from -0.875 to 0.875
- b_o: bfloat16 [384], P('shard'), may hold values from -3 to 3
- w_1: bfloat16 [384, 1536], P('shard'), may hold values from -0.3125 to 0.3125
- b_1: bfloat16 [1536], P('shard'), may hold values from -3 to 3
- w_2: bfloat16 [1536, 384], P('shard'), may hold values from -0.15625 to 0.15625
- b_2: bfloat16 [384], P('shard'), may hold values from -3 to 3
- grad_out: bfloat16 [256, 256, 384], P(('rep', 'shard')), may hold values from -6 to 6
Outputs:
- block_out: bfloat16 [256, 256, 384], P(('rep', 'shard'))
- grad_tokens: float32 [256, 256, 384], P(('rep', 'shard'))
- grad_cond: float32 [256, 384], P(('rep', 'shard'))
- grad_w_ada: float32 [384, 2304], P('shard')
- grad_b_ada: float32 [2304], P('shard')
- grad_w_qkv: float32 [384, 1152], P('shard')
- grad_b_qv: float32 [768], P('shard')
- grad_w_o: float32 [384, 384], P('shard')
- grad_b_o: float32 [384], P('shard')
- grad_w_1: float32 [384, 1536], P('shard')
- grad_b_1: float32 [1536], P('shard')
- grad_w_2: float32 [1536, 384], P('shard')
- grad_b_2: float32 [384], P('shard')
All inputs are finite; a program needn't handle non-finite values.
Results may differ from a plain program's by a relative error of at most 0.019.
The roundings to bfloat16 on the way count: a program that leaves them out, or rounds other values in their place, can miss the bound.
Values may be sent and summed in bfloat16 or wider, within the bound.
No kernel may reach another device: no remote copies, remote signals or barrier semaphores. Data moves between devices by JAX's collectives and lax.ppermute only.
A program may use at most 128 MiB of HBM per device.

v0:
```python
import math
import jax
import jax.numpy as jnp
from jax import lax
from jax.sharding import PartitionSpec as P

HEADS = 6


def layer_norm(value):
    centred = value - jnp.mean(value, axis=-1, keepdims=True)
    factor = lax.rsqrt(jnp.mean(centred * centred, axis=-1, keepdims=True) + 1e-06)
    return (centred * factor, factor)


def norm_back(normed, factor, grad_normed):
    inner = jnp.mean(grad_normed, axis=-1, keepdims=True)
    along = jnp.mean(grad_normed * normed, axis=-1, keepdims=True)
    return factor * (grad_normed - inner - normed * along)


def project(left, right):
    return jnp.einsum("lsd,de->lse", left, right, preferred_element_type=jnp.float32)


def weight_grad(left, right):
    return jnp.einsum("lsd,lse->de", left, right, preferred_element_type=jnp.float32)


def attend(items):
    query, key, value = items
    scores = jnp.einsum("lqhd,lkhd->lhqk", query, key, preferred_element_type=jnp.float32) * 0.125
    top = jnp.max(scores, axis=-1, keepdims=True)
    expo = jnp.exp(scores - top)
    total = jnp.sum(expo, axis=-1, keepdims=True)
    probs = (expo / total).astype(jnp.bfloat16)
    attended = jnp.einsum("lhqk,lkhd->lqhd", probs, value, preferred_element_type=jnp.float32)
    return (attended.astype(jnp.bfloat16), top + jnp.log(total))


def attend_back(items):
    query, key, value, logsum, grad_att = items
    scores = jnp.einsum("lqhd,lkhd->lhqk", query, key, preferred_element_type=jnp.float32) * 0.125
    probs = jnp.exp(scores - logsum)
    rounded = probs.astype(jnp.bfloat16)
    grad_value = jnp.einsum(
        "lhqk,lqhd->lkhd", rounded, grad_att, preferred_element_type=jnp.float32
    )
    grad_probs = jnp.einsum("lqhd,lkhd->lhqk", grad_att, value, preferred_element_type=jnp.float32)
    row_total = jnp.sum(probs * grad_probs, axis=-1, keepdims=True)
    grad_scores = (probs * (grad_probs - row_total)).astype(jnp.bfloat16)
    grad_query = (
        jnp.einsum("lhqk,lkhd->lqhd", grad_scores, key, preferred_element_type=jnp.float32) * 0.125
    )
    grad_key = (
        jnp.einsum("lhqk,lqhd->lkhd", grad_scores, query, preferred_element_type=jnp.float32)
        * 0.125
    )
    return (
        grad_query.astype(jnp.bfloat16),
        grad_key.astype(jnp.bfloat16),
        grad_value.astype(jnp.bfloat16),
    )


def on_device(
    latent_tokens, cond, w_ada, b_ada, w_qkv, b_qv, w_o, b_o, w_1, b_1, w_2, b_2, grad_out
):
    count, length, width = latent_tokens.shape
    head_size = width // HEADS
    per_block = math.gcd(count, max(1, 512 // length))
    blocks = count // per_block
    whole = (
        lax.all_gather(w_ada, "shard", axis=0, tiled=True),
        lax.all_gather(b_ada, "shard", axis=0, tiled=True),
        lax.all_gather(w_qkv, "shard", axis=0, tiled=True),
        lax.all_gather(b_qv, "shard", axis=0, tiled=True),
        lax.all_gather(w_o, "shard", axis=0, tiled=True),
        lax.all_gather(b_o, "shard", axis=0, tiled=True),
        lax.all_gather(w_1, "shard", axis=0, tiled=True),
        lax.all_gather(b_1, "shard", axis=0, tiled=True),
        lax.all_gather(w_2, "shard", axis=0, tiled=True),
        lax.all_gather(b_2, "shard", axis=0, tiled=True),
    )
    f_ada, f_bada, f_qkv, f_bqv, f_wo, f_bo, f_w1, f_b1, f_w2, f_b2 = whole
    tokens = latent_tokens.astype(jnp.float32)
    condition = cond.astype(jnp.float32)
    cs = jax.nn.silu(condition).astype(jnp.bfloat16)
    ada = jnp.dot(cs, f_ada, preferred_element_type=jnp.float32) + f_bada.astype(jnp.float32)
    shift1, scale1, gate1, shift2, scale2, gate2 = jnp.split(ada, 6, axis=-1)
    n1, rstd1 = layer_norm(tokens)
    m1 = (n1 * (1.0 + scale1[:, None]) + shift1[:, None]).astype(jnp.bfloat16)
    qkv = project(m1, f_qkv)
    bias_qv = f_bqv.astype(jnp.float32)
    query = (qkv[..., :width] + bias_qv[:width]).astype(jnp.bfloat16)
    key = qkv[..., width : 2 * width].astype(jnp.bfloat16)
    value = (qkv[..., 2 * width :] + bias_qv[width:]).astype(jnp.bfloat16)
    shape_blocks = (blocks, per_block, length, HEADS, head_size)
    q_blocks = query.reshape(shape_blocks)
    k_blocks = key.reshape(shape_blocks)
    v_blocks = value.reshape(shape_blocks)
    att_blocks, logsum = lax.map(attend, (q_blocks, k_blocks, v_blocks))
    attended = att_blocks.reshape(count, length, width)
    branch = project(attended, f_wo) + f_bo.astype(jnp.float32)
    x1 = tokens + gate1[:, None] * branch
    n2, rstd2 = layer_norm(x1)
    m2 = (n2 * (1.0 + scale2[:, None]) + shift2[:, None]).astype(jnp.bfloat16)
    hidden = project(m2, f_w1) + f_b1.astype(jnp.float32)
    gelu_out, gelu_vjp = jax.vjp(lambda t: jax.nn.gelu(t, approximate=True), hidden)
    gelu_low = gelu_out.astype(jnp.bfloat16)
    ffn = project(gelu_low, f_w2) + f_b2.astype(jnp.float32)
    block_out = (x1 + gate2[:, None] * ffn).astype(jnp.bfloat16)
    again = (
        lax.all_gather(w_ada, "shard", axis=0, tiled=True),
        lax.all_gather(w_qkv, "shard", axis=0, tiled=True),
        lax.all_gather(w_o, "shard", axis=0, tiled=True),
        lax.all_gather(w_1, "shard", axis=0, tiled=True),
        lax.all_gather(w_2, "shard", axis=0, tiled=True),
    )
    g_ada, g_qkv, g_wo, g_w1, g_w2 = again
    cotangent = grad_out.astype(jnp.float32)
    grad_ffn = (cotangent * gate2[:, None]).astype(jnp.bfloat16)
    d_gate2 = jnp.sum(cotangent * ffn, axis=1)
    gw_2 = weight_grad(gelu_low, grad_ffn)
    gb_2 = jnp.sum(grad_ffn.astype(jnp.float32), axis=(0, 1))
    grad_gelu = jnp.einsum("lse,de->lsd", grad_ffn, g_w2, preferred_element_type=jnp.float32)
    grad_hidden = gelu_vjp(grad_gelu)[0].astype(jnp.bfloat16)
    gw_1 = weight_grad(m2, grad_hidden)
    gb_1 = jnp.sum(grad_hidden.astype(jnp.float32), axis=(0, 1))
    grad_m2 = jnp.einsum("lse,de->lsd", grad_hidden, g_w1, preferred_element_type=jnp.float32)
    d_scale2 = jnp.sum(grad_m2 * n2, axis=1)
    d_shift2 = jnp.sum(grad_m2, axis=1)
    grad_x1 = cotangent + norm_back(n2, rstd2, grad_m2 * (1.0 + scale2[:, None]))
    grad_branch = (grad_x1 * gate1[:, None]).astype(jnp.bfloat16)
    d_gate1 = jnp.sum(grad_x1 * branch, axis=1)
    gw_o = weight_grad(attended, grad_branch)
    gb_o = jnp.sum(grad_branch.astype(jnp.float32), axis=(0, 1))
    grad_att = jnp.einsum(
        "lse,de->lsd", grad_branch, g_wo, preferred_element_type=jnp.float32
    ).astype(jnp.bfloat16)
    dq, dk, dv = lax.map(
        attend_back, (q_blocks, k_blocks, v_blocks, logsum, grad_att.reshape(shape_blocks))
    )
    grad_qkv = jnp.concatenate(
        [
            dq.reshape(count, length, width),
            dk.reshape(count, length, width),
            dv.reshape(count, length, width),
        ],
        axis=-1,
    )
    gw_qkv = weight_grad(m1, grad_qkv)
    column_sums = jnp.sum(grad_qkv.astype(jnp.float32), axis=(0, 1))
    gb_qv = jnp.concatenate([column_sums[:width], column_sums[2 * width :]])
    grad_m1 = jnp.einsum("lse,de->lsd", grad_qkv, g_qkv, preferred_element_type=jnp.float32)
    d_scale1 = jnp.sum(grad_m1 * n1, axis=1)
    d_shift1 = jnp.sum(grad_m1, axis=1)
    grad_tokens = grad_x1 + norm_back(n1, rstd1, grad_m1 * (1.0 + scale1[:, None]))
    grad_ada = jnp.concatenate(
        [d_shift1, d_scale1, d_gate1, d_shift2, d_scale2, d_gate2], axis=-1
    ).astype(jnp.bfloat16)
    gw_ada = jnp.dot(cs.T, grad_ada, preferred_element_type=jnp.float32)
    gb_ada = jnp.sum(grad_ada.astype(jnp.float32), axis=0)
    grad_cs = jnp.dot(grad_ada, g_ada.T, preferred_element_type=jnp.float32)
    silu_grad = jax.vjp(jax.nn.silu, condition)[1](grad_cs)[0]
    partial_value = (
        lax.psum_scatter(
            gw_ada.astype(jnp.bfloat16), "shard", scatter_dimension=0, tiled=True
        ).astype(jnp.float32),
        lax.psum_scatter(
            gb_ada.astype(jnp.bfloat16), "shard", scatter_dimension=0, tiled=True
        ).astype(jnp.float32),
        lax.psum_scatter(
            gw_qkv.astype(jnp.bfloat16), "shard", scatter_dimension=0, tiled=True
        ).astype(jnp.float32),
        lax.psum_scatter(
            gb_qv.astype(jnp.bfloat16), "shard", scatter_dimension=0, tiled=True
        ).astype(jnp.float32),
        lax.psum_scatter(
            gw_o.astype(jnp.bfloat16), "shard", scatter_dimension=0, tiled=True
        ).astype(jnp.float32),
        lax.psum_scatter(
            gb_o.astype(jnp.bfloat16), "shard", scatter_dimension=0, tiled=True
        ).astype(jnp.float32),
        lax.psum_scatter(
            gw_1.astype(jnp.bfloat16), "shard", scatter_dimension=0, tiled=True
        ).astype(jnp.float32),
        lax.psum_scatter(
            gb_1.astype(jnp.bfloat16), "shard", scatter_dimension=0, tiled=True
        ).astype(jnp.float32),
        lax.psum_scatter(
            gw_2.astype(jnp.bfloat16), "shard", scatter_dimension=0, tiled=True
        ).astype(jnp.float32),
        lax.psum_scatter(
            gb_2.astype(jnp.bfloat16), "shard", scatter_dimension=0, tiled=True
        ).astype(jnp.float32),
    )
    summed = (
        lax.psum(partial_value[0].astype(jnp.bfloat16), "rep").astype(jnp.float32),
        lax.psum(partial_value[1].astype(jnp.bfloat16), "rep").astype(jnp.float32),
        lax.psum(partial_value[2].astype(jnp.bfloat16), "rep").astype(jnp.float32),
        lax.psum(partial_value[3].astype(jnp.bfloat16), "rep").astype(jnp.float32),
        lax.psum(partial_value[4].astype(jnp.bfloat16), "rep").astype(jnp.float32),
        lax.psum(partial_value[5].astype(jnp.bfloat16), "rep").astype(jnp.float32),
        lax.psum(partial_value[6].astype(jnp.bfloat16), "rep").astype(jnp.float32),
        lax.psum(partial_value[7].astype(jnp.bfloat16), "rep").astype(jnp.float32),
        lax.psum(partial_value[8].astype(jnp.bfloat16), "rep").astype(jnp.float32),
        lax.psum(partial_value[9].astype(jnp.bfloat16), "rep").astype(jnp.float32),
    )
    return (
        block_out,
        grad_tokens,
        silu_grad,
        summed[0],
        summed[1],
        summed[2],
        summed[3],
        summed[4],
        summed[5],
        summed[6],
        summed[7],
        summed[8],
        summed[9],
    )


def solution(mesh):
    in_specs = (
        P(("rep", "shard"), None, None),
        P(("rep", "shard"), None),
        P("shard", None),
        P("shard"),
        P("shard", None),
        P("shard"),
        P("shard", None),
        P("shard"),
        P("shard", None),
        P("shard"),
        P("shard", None),
        P("shard"),
        P(("rep", "shard"), None, None),
    )
    out_specs = (
        P(("rep", "shard"), None, None),
        P(("rep", "shard"), None, None),
        P(("rep", "shard"), None),
        P("shard", None),
        P("shard"),
        P("shard", None),
        P("shard"),
        P("shard", None),
        P("shard"),
        P("shard", None),
        P("shard"),
        P("shard", None),
        P("shard"),
    )
    return jax.shard_map(
        on_device, mesh=mesh, in_specs=in_specs, out_specs=out_specs, check_vma=False
    )
```

profile of v0, /device:TPU:0, one launch (start us, length us, event | category | flops | bytes accessed | tf_op | source)
XLA Modules:
  0.0 425.0 jit_solution(18000375624998559178)
XLA Ops:
  13.5 6.1 %all-gather = bf16[4,1,384]{2,1,0:T(2,128)(2,1)S(1)} all-gather(bf16[1,1,384]{2,1,0:T(2,128)(2,1)S(1)} %reshape.148), channel_id=1, replica_groups=mesh['rep'=8,'shard'=4] {'shard'}, dimensions={0}, use_global_device_ids=true | all-gather | bytes 3840 | tf_op jit(solution)/shard_map/all_gather | solution.py:81
  23.6 12.3 %all-reduce.12 = (bf16[2304]{0:T(1024)(128)(2,1)S(1)}, bf16[768]{0:T(1024)(128)(2,1)S(1)}, bf16[384]{0:T(512)(128)(2,1)S(1)}, bf16[384]{0:T(512)(128)(2,1)S(1)}) all-reduce(bf16[2304]{0:T(1024)(128)(2,1)S(1)} %dynamic-update-slice, bf16[768]{0:T(1024)(128)(2,1)S(1)} %dynamic-update-slice.1, ...), channel_id=1, replica_groups=mesh['rep'=8,'shard'=4] {'shard'}, use_global_device_ids=true, to_apply=%add | all-reduce | flops 3840 | bytes 15360
  39.2 5.9 %all_gather.39 = bf16[384,384]{1,0:T(8,128)(2,1)S(1)} all-gather(bf16[96,384]{1,0:T(8,128)(2,1)S(1)} %copy-done.16), channel_id=1, replica_groups=mesh['rep'=8,'shard'=4] {'shard'}, dimensions={0}, use_global_device_ids=true | all-gather | bytes 368640 | tf_op jit(solution)/shard_map/all_gather | solution.py:78
  45.1 11.3 %all_gather.37 = bf16[384,1152]{1,0:T(8,128)(2,1)S(1)} all-gather(bf16[96,1152]{1,0:T(8,128)(2,1)S(1)} %copy-done.15), channel_id=1, replica_groups=mesh['rep'=8,'shard'=4] {'shard'}, dimensions={0}, use_global_device_ids=true | all-gather | bytes 1105920 | tf_op jit(solution)/shard_map/all_gather | solution.py:76
  56.4 2.1 convolution_add_fusion
  59.2 3.0 fusion.98
  63.5 2.4 fusion.80
  67.6 2.6 copy.80
  70.2 2.6 copy.78
  74.2 18.9 %while.26 = (s32[]{:T(128)}, bf16[4,2,256,6,64]{2,4,3,1,0:T(8,128)(2,1)}, f32[4,2,6,256,1]{3,2,1,4,0:T(8,128)S(1)}, bf16[4,2,256,6,64]{2,4,3,1,0:T(8,128)(2,1)},...) while((s32[]{:T(128)}, ...), condition=%wide.region_5.6_spmd, body=%wide.region_2.5_spmd.sunk | while | flops 208598016 | bytes 11122777 | solution.py:102
  76.3 2.5 fusion.152
  81.1 2.5 fusion.152
  85.8 2.5 fusion.152
  90.6 2.5 fusion.152
  93.1 4.6 %fusion.115 = (f32[8,256]{1,0:T(8,128)S(1)}, f32[8,256,384]{2,1,0:T(8,128)S(1)}, f32[8,256,384]{2,1,0:T(8,128)}) fusion(f32[384]{0:T(512)S(1)} %convert_element_type.177, f32[8,384]{1,0:T(8,128)S(1)} %get-tuple-element.197, bf16[8,256,384]{2,1,0:T(8,128)(2,1)S(1)} %copy-done, bf16[8,256,384]{1,2,0:T(8,128)(2,1)} %bitcast.178, ...), kind=kOutput, calls=%fused_computation.164 | convolution fusion | flops 607909888 | bytes 9754112 | tf_op jit(solution)/shard_map/lsd,de->lse/dot_general | solution.py:23
  100.7 11.0 %multiply_convert_fusion.1 = (bf16[8,256,1536]{2,1,0:T(8,128)(2,1)}, f32[8,256,1536]{2,1,0:T(8,128)}) fusion(f32[1536]{0:T(1024)} %reshape.150, bf16[384,1536]{1,0:T(8,128)(2,1)} %all-gather.7.cloned.1.call-done, f32[8,256,384]{2,1,0:T(8,128)} %copy-done.1, f32[8,384]{1,0:T(8,128)} %get-tuple-element.193, f32[8,384]{1,0:T(8,128)} %get-tuple-element.194, ...), kind=kOutput, calls=%fused_computation.69 | convolution fusion | flops 2451308544 | bytes 23246848 | tf_op jit(solution)/shard_map/lsd,de->lse/dot_general | solution.py:23
  111.7 15.0 %fusion.120 = (bf16[1536]{0:T(1024)(128)(2,1)}, bf16[8,256,1536]{2,1,0:T(8,128)(2,1)S(1)}) fusion(f32[8,256,1536]{2,1,0:T(8,128)} %get-tuple-element.206, f32[1536]{0:T(1024)} %reshape.150, bf16[1536,384]{1,0:T(8,128)(2,1)} %all-gather.9.cloned.1.call-done, bf16[8,256,384]{2,1,0:T(8,128)(2,1)} %param.29, f32[8,384]{1,0:T(8,128)} %get-tuple-element.192), kind=kOutput, calls=%fused_computation.169 | convolution fusion | flops 2487482880 | bytes 21648384 | tf_op jit(solution)/shard_map/lse,de->lsd/dot_general | solution.py:126
  126.9 3.6 fusion.92
  131.8 1.9 copy-done.40
  133.7 6.0 %fusion.79 = (bf16[8,384]{1,0:T(8,128)(2,1)}, bf16[8,256,384]{2,1,0:T(8,128)(2,1)}, bf16[8,384]{1,0:T(8,128)(2,1)}, f32[8,256]{1,0:T(8,128)S(1)}, f32[8,256]{1,0:T(8,128)S(1)}, /*index=5*/bf16[8,384]{1,0:T(8,128)(2,1)}) fusion(bf16[8,256,384]{2,1,0:T(8,128)(2,1)S(1)} %copy-done.13, f32[384]{0:T(512)S(1)} %copy-done.36, f32[8,256,384]{2,1,0:T(8,128)S(1)} %copy-done.2, ...), kind=kOutput, calls=%fused_computation.94 | convolution fusion | flops 2428488704 | bytes 16985600 | tf_op jit(solution)/shard_map/lsd,de->lse/dot_general | solution.py:23
  139.7 4.1 fusion.114
  146.6 3.7 convolution_convert_fusion.1
  150.4 2.6 copy.82
  157.0 37.3 %while.27 = (s32[]{:T(128)}, bf16[4,2,256,6,64]{2,4,3,1,0:T(8,128)(2,1)}, bf16[4,2,256,6,64]{2,4,3,1,0:T(8,128)(2,1)}, bf16[4,2,256,6,64]{2,4,3,1,0:T(8,128)(2,1...) while((s32[]{:T(128)}, ...), condition=%wide.region_12.13_spmd, body=%wide.region_10.12_spmd.sunk | while | flops 513733632 | bytes 33916044 | solution.py:141
  160.2 1.9 multiply_reduce_fusion.11
  164.2 2.1 fusion.162
  169.5 1.9 multiply_reduce_fusion.11
  173.5 2.1 fusion.162
  178.8 1.9 multiply_reduce_fusion.11
  182.8 2.1 fusion.162
  188.2 1.9 multiply_reduce_fusion.11
  192.2 2.1 fusion.162
  194.3 2.7 copy.85
  197.1 2.6 copy.83
  201.3 6.2 %fusion.82 = bf16[384,1152]{1,0:T(8,128)(2,1)} fusion(bf16[8,256,384]{2,1,0:T(8,128)(2,1)S(1)} %copy-done, f32[8,384]{1,0:T(8,128)S(1)} %copy-done.24, f32[8,384]{1,0:T(8,128)S(1)} %get-tuple-element.196, f32[8,256]{1,0:T(8,128)S(1)} %add_rsqrt_fusion.1, f32[8,256]{1,0:T(8,128)S(1)} %broadcast_multiply_fusion.5, bf16[8,256,384]{2,1,0:T(8,128)(2,1)} %copy.85, ...), kind=kOutput, calls=%fused_computation.111 | convolution fusion | flops 1831256064 | bytes 7217152 | tf_op jit(solution)/shard_map/lsd,lse->de/dot_general | solution.py:27
  207.6 7.6 %fusion.83 = bf16[384,1536]{1,0:T(8,128)(2,1)} fusion(bf16[8,256,1536]{2,1,0:T(8,128)(2,1)} %copy-done.39, f32[8,256,384]{2,1,0:T(8,128)} %copy-done.1, f32[8,384]{1,0:T(8,128)S(1)} %copy-done.29, f32[8,384]{1,0:T(8,128)S(1)} %copy-done.22, f32[8,256]{1,0:T(8,128)S(1)} %copy-done.26, f32[8,256]{1,0:T(8,128)S(1)} %broadcast_multiply_fusion.4), kind=kOutput, calls=%fused_computation.112 | convolution fusion | flops 2420441088 | bytes 10657792 | tf_op jit(solution)/shard_map/lsd,lse->de/dot_general | solution.py:27
  215.5 8.0 %fusion.84 = bf16[1536,384]{1,0:T(8,128)(2,1)} fusion(bf16[8,256,1536]{2,1,0:T(8,128)(2,1)} %get-tuple-element.205, bf16[8,256,384]{2,1,0:T(8,128)(2,1)} %param.29, f32[8,384]{1,0:T(8,128)S(1)} %copy-done.20), kind=kOutput, calls=%fused_computation.113 | convolution fusion | flops 2418868224 | bytes 9056256 | tf_op jit(solution)/shard_map/lsd,lse->de/dot_general | solution.py:27
  223.6 6.2 %fusion.76 = (bf16[8,384]{1,0:T(8,128)(2,1)S(1)}, f32[8,256]{1,0:T(8,128)S(1)}, f32[8,256]{1,0:T(8,128)S(1)}, bf16[8,384]{1,0:T(8,128)(2,1)S(1)}, f32[8,256,384]{2,1,0:T(8,128)S(1)}) fusion(bf16[8,256,384]{2,1,0:T(8,128)(2,1)S(1)} %copy-done, f32[8,256]{1,0:T(8,128)S(1)} %add_rsqrt_fusion.1, f32[8,256]{1,0:T(8,128)S(1)} %broadcast_multiply_fusion.5, ...), kind=kOutput, calls=%fused_computation.91 | convolution fusion | flops 1833949184 | bytes 10379264 | tf_op jit(solution)/shard_map/lse,de->lsd/dot_general | solution.py:155
  229.9 3.1 multiply_reduce_fusion.3
  233.1 1.9 convolution_convert_fusion
  235.2 24.6 %reduce-scatter.12.cloned.1.call-done = bf16[96,1536]{1,0:T(8,128)(2,1)} async-done(((bf16[384,1536]{1,0:T(8,128)(2,1)}), bf16[96,1536]{1,0:T(8,128)(2,1)}) %reduce-scatter.12.cloned.1.call-update) | async-done | bytes 294928 | tf_op jit(solution)/shard_map/reduce_scatter | solution.py:185
  259.8 28.5 %reduce-scatter.14.cloned.1.call-done = bf16[384,384]{1,0:T(8,128)(2,1)} async-done(((bf16[1536,384]{1,0:T(8,128)(2,1)}), bf16[384,384]{1,0:T(8,128)(2,1)}) %reduce-scatter.14.cloned.1.call-update) | async-done | bytes 294928 | tf_op jit(solution)/shard_map/reduce_scatter | solution.py:191
  288.3 32.0 %reduce-scatter.6.cloned.1.call-done = bf16[96,2304]{1,0:T(8,128)(2,1)} async-done(((bf16[384,2304]{1,0:T(8,128)(2,1)}), bf16[96,2304]{1,0:T(8,128)(2,1)}) %reduce-scatter.6.cloned.1.call-update) | async-done | bytes 442384 | tf_op jit(solution)/shard_map/reduce_scatter | solution.py:167
  322.9 2.3 fusion.113
  325.2 10.5 %all-reduce.11 = (bf16[2304]{0:T(1024)(128)(2,1)S(1)}, bf16[768]{0:T(1024)(128)(2,1)S(1)}, bf16[384]{0:T(512)(128)(2,1)S(1)}, bf16[1536]{0:T(1024)(128)(2,1)S(1)}, bf16[384]{0:T(512)(128)(2,1)S(1)}) all-reduce(bf16[2304]{0:T(1024)(128)(2,1)S(1)} %reduce_sum.215, ...), channel_id=3, replica_groups=mesh['rep'=8,'shard'=4] {'shard'}, use_global_device_ids=true, to_apply=%region_24.25.clone | all-reduce | flops 5376 | bytes 21504
  336.1 22.2 %all-reduce.9 = (bf16[576]{0:T(1024)(128)(2,1)S(1)}, bf16[192]{0:T(256)(128)(2,1)S(1)}, bf16[96]{0:T(256)(128)(2,1)S(1)}, bf16[384]{0:T(512)(128)(2,1)S(1)}, bf16[96]{0:T(256)(128)(2,1)S(1)}) all-reduce(bf16[576]{0:T(1024)(128)(2,1)S(1)} %dynamic-slice.5, ...), channel_id=1, replica_groups=mesh['rep'=8,'shard'=4] {'rep'}, use_global_device_ids=true, to_apply=%region_25.26 | all-reduce | flops 1344 | bytes 5376 | tf_op jit(solution)/shard_map/psum | solution.py:200
  362.3 47.9 %all-reduce.15.cloned.1.call-done = (bf16[96,2304]{1,0:T(8,128)(2,1)}, bf16[96,1152]{1,0:T(8,128)(2,1)}, bf16[96,384]{1,0:T(8,128)(2,1)}, bf16[96,1536]{1,0:T(8,128)(2,1)}, bf16[384,384]{1,0:T(8,128)(2,1)}) async-done(((bf16[96,2304]{1,0:T(8,128)(2,1)}, bf16[96,1152]{1,0:T(8,128)(2,1)}, bf16[96,384]{1,0:T(8,128)(2,1)}, bf16[96,1536]{1,0:T(8,128)(2,1)}, bf16[384,384]{1,0:T(8,128)(2,1)}), ...) | async-done | bytes 1327120 | tf_op jit(solution)/shard_map/psum | solution.py:199
  411.8 2.0 convert_element_type.189
  (202 shorter events, 70.3 us)
Async XLA Ops:
  7.2 31.1 %copy-start = (bf16[8,256,384]{2,1,0:T(8,128)(2,1)S(1)}, bf16[8,256,384]{2,1,0:T(8,128)(2,1)}, u32[]{:S(2)}) copy-start(bf16[8,256,384]{2,1,0:T(8,128)(2,1)} %param.17) | copy-start | bytes 4718596
  7.2 32.0 %copy-start.16 = (bf16[96,384]{1,0:T(8,128)(2,1)S(1)}, bf16[96,384]{1,0:T(8,128)(2,1)}, u32[]{:S(2)}) copy-start(bf16[96,384]{1,0:T(8,128)(2,1)} %param.23) | copy-start | bytes 221188
  7.2 37.9 %copy-start.15 = (bf16[96,1152]{1,0:T(8,128)(2,1)S(1)}, bf16[96,1152]{1,0:T(8,128)(2,1)}, u32[]{:S(2)}) copy-start(bf16[96,1152]{1,0:T(8,128)(2,1)} %param.21) | copy-start | bytes 663556
  7.2 49.2 %copy-start.17 = (bf16[8,384]{1,0:T(8,128)(2,1)S(1)}, bf16[8,384]{1,0:T(8,128)(2,1)}, u32[]{:S(2)}) copy-start(bf16[8,384]{1,0:T(8,128)(2,1)} %param.18) | copy-start | bytes 18436
  7.2 49.2 %all-gather.5.cloned.1.call-start = ((), (), s32[]{:S(2)}) async-start(), calls=%async_computation.5 | async-start | bytes 2211840 | tf_op jit(solution)/shard_map/all_gather | solution.py:74
  8.0 92.7 %all-gather.7.cloned.1.call-start = ((), (), s32[]{:S(2)}) async-start(), calls=%async_computation.6 | async-start | bytes 1474560 | tf_op jit(solution)/shard_map/all_gather | solution.py:80
  8.7 103.0 %all-gather.9.cloned.1.call-start = ((), (), s32[]{:S(2)}) async-start(), calls=%async_computation.7 | async-start | bytes 1474560 | tf_op jit(solution)/shard_map/all_gather | solution.py:82
  9.4 225.7 %reduce-scatter.10.cloned.1.call-start = ((), (), s32[]{:S(2)}) async-start(), calls=%async_computation.10 | async-start | bytes 368640 | tf_op jit(solution)/shard_map/reduce_scatter | solution.py:179
  35.9 57.2 %copy-start.27 = (f32[384]{0:T(512)}, f32[384]{0:T(512)S(1)}, u32[]{:S(2)}) copy-start(f32[384]{0:T(512)S(1)} %convert_element_type.177) | copy-start | bytes 4612
  56.4 5.8 %copy-start.12 = (bf16[384,1152]{1,0:T(8,128)(2,1)}, bf16[384,1152]{1,0:T(8,128)(2,1)S(1)}, u32[]{:S(2)}) copy-start(bf16[384,1152]{1,0:T(8,128)(2,1)S(1)} %all_gather.37) | copy-start | bytes 2654212
  59.2 3.0 copy-start.23
  111.7 15.1 %copy-start.38 = (bf16[384,1536]{1,0:T(8,128)(2,1)S(1)}, bf16[384,1536]{1,0:T(8,128)(2,1)}, u32[]{:S(2)}) copy-start(bf16[384,1536]{1,0:T(8,128)(2,1)} %all-gather.7.cloned.1.call-done) | copy-start | bytes 3538948
  126.8 3.7 copy-start.39
  126.8 4.2 copy-start.2
  126.8 4.6 %copy-start.13 = (bf16[8,256,384]{2,1,0:T(8,128)(2,1)S(1)}, bf16[8,256,384]{2,1,0:T(8,128)(2,1)}, u32[]{:S(2)}) copy-start(bf16[8,256,384]{2,1,0:T(8,128)(2,1)} %param.29) | copy-start | bytes 4718596
  126.8 4.6 %copy-start.19 = (f32[8,384]{1,0:T(8,128)S(1)}, f32[8,384]{1,0:T(8,128)}, u32[]{:S(2)}) copy-start(f32[8,384]{1,0:T(8,128)} %get-tuple-element.192) | copy-start | bytes 36868
  126.8 4.6 %copy-start.21 = (f32[8,384]{1,0:T(8,128)S(1)}, f32[8,384]{1,0:T(8,128)}, u32[]{:S(2)}) copy-start(f32[8,384]{1,0:T(8,128)} %get-tuple-element.194) | copy-start | bytes 36868
  126.8 4.6 %copy-start.25 = (f32[8,256]{1,0:T(8,128)S(1)}, f32[8,256]{1,0:T(8,128)}, u32[]{:S(2)}) copy-start(f32[8,256]{1,0:T(8,128)} %add_rsqrt_fusion) | copy-start | bytes 24580
  126.8 4.6 %copy-start.36 = (f32[384]{0:T(512)S(1)}, f32[384]{0:T(512)}, u32[]{:S(2)}) copy-start(f32[384]{0:T(512)} %convert_element_type.181) | copy-start | bytes 4612
  126.8 5.0 %copy-start.37 = (bf16[1536,384]{1,0:T(8,128)(2,1)S(1)}, bf16[1536,384]{1,0:T(8,128)(2,1)}, u32[]{:S(2)}) copy-start(bf16[1536,384]{1,0:T(8,128)(2,1)} %all-gather.9.cloned.1.call-done) | copy-start | bytes 3538948
  126.8 6.8 %copy-start.40 = (bf16[8,256,1536]{2,1,0:T(8,128)(2,1)S(1)}, bf16[8,256,1536]{2,1,0:T(8,128)(2,1)}, u32[]{:S(2)}) copy-start(bf16[8,256,1536]{2,1,0:T(8,128)(2,1)} %get-tuple-element.205) | copy-start | bytes 18874372
  139.7 5.2 %copy-start.9 = (bf16[4,2,256,6,64]{2,4,3,1,0:T(8,128)(2,1)S(1)}, bf16[4,2,256,6,64]{2,4,3,1,0:T(8,128)(2,1)}, u32[]{:S(2)}) copy-start(bf16[4,2,256,6,64]{2,4,3,1,0:T(8,128)(2,1)} %get-tuple-element.95) | copy-start | bytes 4718596
  150.3 84.8 %reduce-scatter.8.cloned.1.call-start = ((), (), s32[]{:S(2)}) async-start(), calls=%async_computation.9 | async-start | bytes 1105920 | tf_op jit(solution)/shard_map/reduce_scatter | solution.py:173
  157.0 1.7 copy-start.3
  194.3 5.3 %copy-start.8 = (bf16[4,2,256,6,64]{2,4,3,1,0:T(8,128)(2,1)S(1)}, bf16[4,2,256,6,64]{2,4,3,1,0:T(8,128)(2,1)}, u32[]{:S(2)}) copy-start(bf16[4,2,256,6,64]{2,4,3,1,0:T(8,128)(2,1)} %get-tuple-element.98) | copy-start | bytes 4718596
  197.1 4.2 copy-start.24
  201.3 6.3 %copy-start.22 = (f32[8,384]{1,0:T(8,128)S(1)}, f32[8,384]{1,0:T(8,128)}, u32[]{:S(2)}) copy-start(f32[8,384]{1,0:T(8,128)} %get-tuple-element.194) | copy-start | bytes 36868
  201.3 6.3 %copy-start.26 = (f32[8,256]{1,0:T(8,128)S(1)}, f32[8,256]{1,0:T(8,128)}, u32[]{:S(2)}) copy-start(f32[8,256]{1,0:T(8,128)} %add_rsqrt_fusion) | copy-start | bytes 24580
  201.3 6.3 %copy-start.29 = (f32[8,384]{1,0:T(8,128)S(1)}, f32[8,384]{1,0:T(8,128)}, u32[]{:S(2)}) copy-start(f32[8,384]{1,0:T(8,128)} %get-tuple-element.193) | copy-start | bytes 36868
  207.5 8.0 %copy-start.20 = (f32[8,384]{1,0:T(8,128)S(1)}, f32[8,384]{1,0:T(8,128)}, u32[]{:S(2)}) copy-start(f32[8,384]{1,0:T(8,128)} %get-tuple-element.192) | copy-start | bytes 36868
  207.5 52.3 %reduce-scatter.12.cloned.1.call-start = ((), (), s32[]{:S(2)}) async-start(), calls=%async_computation.11 | async-start | bytes 1474560 | tf_op jit(solution)/shard_map/reduce_scatter | solution.py:185
  215.2 8.3 %copy-start.10 = (bf16[8,256,384]{2,1,0:T(8,128)(2,1)S(1)}, bf16[8,256,384]{2,1,0:T(8,128)(2,1)}, u32[]{:S(2)}) copy-start(bf16[8,256,384]{2,1,0:T(8,128)(2,1)} %copy.85) | copy-start | bytes 4718596
  215.2 73.0 %reduce-scatter.14.cloned.1.call-start = ((), (), s32[]{:S(2)}) async-start(), calls=%async_computation.12 | async-start | bytes 1474560 | tf_op jit(solution)/shard_map/reduce_scatter | solution.py:191
  223.5 6.3 %copy-start.28 = (f32[384]{0:T(512)S(1)}, f32[384]{0:T(512)}, u32[]{:S(2)}) copy-start(f32[384]{0:T(512)} %copy-done.27) | copy-start | bytes 4612
  223.5 96.8 %reduce-scatter.6.cloned.1.call-start = ((), (), s32[]{:S(2)}) async-start(), calls=%async_computation.8 | async-start | bytes 2211840 | tf_op jit(solution)/shard_map/reduce_scatter | solution.py:167
  223.6 6.2 %copy-start.4 = (f32[8,256,384]{2,1,0:T(8,128)S(1)}, f32[8,256,384]{2,1,0:T(8,128)}, u32[]{:S(2)}) copy-start(f32[8,256,384]{2,1,0:T(8,128)} %get-tuple-element.204) | copy-start | bytes 9437188
  223.6 6.2 %copy-start.5 = (f32[8,256,384]{2,1,0:T(8,128)S(1)}, f32[8,256,384]{2,1,0:T(8,128)}, u32[]{:S(2)}) copy-start(f32[8,256,384]{2,1,0:T(8,128)} %get-tuple-element.174) | copy-start | bytes 9437188
  229.8 3.2 copy-start.32
  229.8 3.2 copy-start.31
  229.8 3.2 copy-start.30
  229.9 3.2 copy-start.18
  233.0 89.9 %copy-start.11 = (bf16[8,256,384]{2,1,0:T(8,128)(2,1)S(1)}, bf16[8,256,384]{2,1,0:T(8,128)(2,1)}, u32[]{:S(2)}) copy-start(bf16[8,256,384]{2,1,0:T(8,128)(2,1)} %copy.85) | copy-start | bytes 4718596
  235.0 90.2 %copy-start.33 = (bf16[384]{0:T(512)(128)(2,1)S(1)}, bf16[384]{0:T(512)(128)(2,1)}, u32[]{:S(2)}) copy-start(bf16[384]{0:T(512)(128)(2,1)} %get-tuple-element.172) | copy-start | bytes 2308
  235.0 90.2 %copy-start.34 = (bf16[384]{0:T(512)(128)(2,1)S(1)}, bf16[384]{0:T(512)(128)(2,1)}, u32[]{:S(2)}) copy-start(bf16[384]{0:T(512)(128)(2,1)} %get-tuple-element.191) | copy-start | bytes 2308
  235.0 90.2 %copy-start.35 = (bf16[1536]{0:T(1024)(128)(2,1)S(1)}, bf16[1536]{0:T(1024)(128)(2,1)}, u32[]{:S(2)}) copy-start(bf16[1536]{0:T(1024)(128)(2,1)} %get-tuple-element.208) | copy-start | bytes 9220
  235.0 126.1 %copy-start.6 = (bf16[384,2304]{1,0:T(8,128)(2,1)S(1)}, bf16[384,2304]{1,0:T(8,128)(2,1)}, u32[]{:S(2)}) copy-start(bf16[384,2304]{1,0:T(8,128)(2,1)} %all-gather.5.cloned.1.call-done) | copy-start | bytes 5308420
  235.1 175.2 %all-reduce.15.cloned.1.call-start = ((), (), s32[]{:S(2)}) async-start(), calls=%async_computation.13 | async-start | bytes 2654208 | tf_op jit(solution)/shard_map/psum | solution.py:199
  410.2 7.1 %copy-start.14 = (bf16[384,384]{1,0:T(8,128)(2,1)S(1)}, bf16[384,384]{1,0:T(8,128)(2,1)}, u32[]{:S(2)}) copy-start(bf16[384,384]{1,0:T(8,128)(2,1)} %get-tuple-element.162) | copy-start | bytes 884740
  (5 other events, 8.1 us)
Sparse Core Ops, SparseCore 0:
  9.6 23.5 all-gather.4
  34.8 19.2 all-gather.6
  55.6 17.1 all-gather.8
  150.4 20.4 reduce-scatter.9
  207.6 23.9 reduce-scatter.7
  234.0 25.7 reduce-scatter.11
  262.5 25.7 reduce-scatter.13
  290.9 29.3 reduce-scatter.5
  324.8 85.3 all-reduce.14
where the time goes:
time: 429 us; the launch traced here: 425 us
  waiting for transfers between devices  135 us (31%)
  matrix products  133 us (31%)
  blocking collectives  68.3 us (16%)
  local copies, waits for them, and re-layouts  35.9 us (8%)
  other arithmetic  33 us (8%)
  between operations  19.2 us (4%)
    psum x1, waiting for transfers between devices, on_device(): lax.psum(partial_value[0].astype(jnp.bfloat16), 'rep').astype(jnp.float32)  47.9 us
    reduce_scatter x1, waiting for transfers between devices, on_device(): lax.psum_scatter(gw_ada.astype(jnp.bfloat16), 'shard', scatter_dimension=...  32 us
    reduce_scatter x1, waiting for transfers between devices, on_device(): lax.psum_scatter(gw_2.astype(jnp.bfloat16), 'shard', scatter_dimension=0,...  28.5 us
    dot_general x4, matrix products, project(): jnp.einsum('lsd,de->lse', left, right, preferred_element_type=jnp.float32)  24.6 us
    reduce_scatter x1, waiting for transfers between devices, on_device(): lax.psum_scatter(gw_1.astype(jnp.bfloat16), 'shard', scatter_dimension=0,...  24.6 us
    dot_general x4, matrix products, weight_grad(): jnp.einsum('lsd,lse->de', left, right, preferred_element_type=jnp.float32)  23.4 us
    unnamed x2, blocking collectives  22.9 us
    psum x1, blocking collectives, on_device(): lax.psum(partial_value[1].astype(jnp.bfloat16), 'rep').astype(jnp.float32)  22.2 us
  transfers between devices with their start and end apart: 9, of which 4 were waited for; matrix products, arithmetic and copies ran while one was open for 36% of the time, Pallas kernels for 0%

commit v1 on v0

--- a/solution.py
+++ b/solution.py
@@ -5,6 +5,19 @@
 from jax.sharding import PartitionSpec as P
 
 HEADS = 6
+
+
+def ring_gather(x, axis, dim):
+    ways = lax.axis_size(axis)
+    up = [(d, (d + 1) % ways) for d in range(ways)]
+    down = [(d, (d - 1) % ways) for d in range(ways)]
+    earlier, later = ([x], [x])
+    for _ in range(ways // 2):
+        earlier.append(lax.ppermute(earlier[-1], axis, up))
+    for _ in range((ways - 1) // 2):
+        later.append(lax.ppermute(later[-1], axis, down))
+    line = jnp.concatenate([*earlier[::-1], *later[1:]], axis=dim)
+    return jnp.roll(line, (lax.axis_index(axis) - ways // 2) * x.shape[dim], axis=dim)
 
 
 def layer_norm(value):
@@ -73,7 +86,7 @@
     whole = (
         lax.all_gather(w_ada, "shard", axis=0, tiled=True),
         lax.all_gather(b_ada, "shard", axis=0, tiled=True),
-        lax.all_gather(w_qkv, "shard", axis=0, tiled=True),
+        ring_gather(w_qkv, "shard", 0),
         lax.all_gather(b_qv, "shard", axis=0, tiled=True),
         lax.all_gather(w_o, "shard", axis=0, tiled=True),
         lax.all_gather(b_o, "shard", axis=0, tiled=True),

time: 429 us -> 451 us (1.051)
  waiting for transfers between devices: 135 us -> 151 us
    ppermute x0 -> x3, waiting for transfers between devices: none -> 6.86 us  [the longest x2 6.86 us: ring_gather(): earlier.append(lax.ppermute(earlier[-1], axis, up))]
    reduce_scatter x1, waiting for transfers between devices: 0.02 us -> 5.56 us  [on_device(): lax.psum_scatter(gw_qkv.astype(jnp.bfloat16), 'shard', scatter_dimension=...]
    unnamed x100 -> x107, local copies, waits for them, and re-layouts: 12 us -> 15.1 us
  transfers between devices with their start and end apart: 9 -> 12, of which waited for: 4 -> 6; matrix products, arithmetic and copies ran while one was open for 36% -> 24% of each run, Pallas kernels for 0% -> 0%
where the time goes in v1:
time: 451 us; the launch traced here: 444 us
  waiting for transfers between devices  151 us (33%)
  matrix products  132 us (29%)
  blocking collectives  66.4 us (15%)
  local copies, waits for them, and re-layouts  39.9 us (9%)
  other arithmetic  32.3 us (7%)
  between operations  19.4 us (4%)
    psum x1, waiting for transfers between devices, on_device(): lax.psum(partial_value[0].astype(jnp.bfloat16), 'rep').astype(jnp.float32)  48 us
    reduce_scatter x1, waiting for transfers between devices, on_device(): lax.psum_scatter(gw_ada.astype(jnp.bfloat16), 'shard', scatter_dimension=...  32 us
    reduce_scatter x1, waiting for transfers between devices, on_device(): lax.psum_scatter(gw_2.astype(jnp.bfloat16), 'shard', scatter_dimension=0,...  28.5 us
    reduce_scatter x1, waiting for transfers between devices, on_device(): lax.psum_scatter(gw_1.astype(jnp.bfloat16), 'shard', scatter_dimension=0,...  28.2 us
    dot_general x4, matrix products, project(): jnp.einsum('lsd,de->lse', left, right, preferred_element_type=jnp.float32)  25.9 us
    dot_general x4, matrix products, weight_grad(): jnp.einsum('lsd,lse->de', left, right, preferred_element_type=jnp.float32)  23.8 us
    psum x1, blocking collectives, on_device(): lax.psum(partial_value[1].astype(jnp.bfloat16), 'rep').astype(jnp.float32)  22.2 us
    unnamed x2, blocking collectives  22.1 us
  transfers between devices with their start and end apart: 12, of which 6 were waited for; matrix products, arithmetic and copies ran while one was open for 24% of the time, Pallas kernels for 0%

profile of v1, /device:TPU:0, one launch (start us, length us, event | category | flops | bytes accessed | tf_op | source)
XLA Modules:
  0.0 444.3 jit_solution(2811673916843557214)
XLA Ops:
  9.3 2.0 collective-permute-start.2
  18.1 11.6 %all-reduce.12 = (bf16[2304]{0:T(1024)(128)(2,1)S(1)}, bf16[768]{0:T(1024)(128)(2,1)S(1)}, bf16[384]{0:T(512)(128)(2,1)S(1)}, bf16[384]{0:T(512)(128)(2,1)S(1)}) all-reduce(bf16[2304]{0:T(1024)(128)(2,1)S(1)} %dynamic-update-slice, bf16[768]{0:T(1024)(128)(2,1)S(1)} %dynamic-update-slice.1, ...), channel_id=1, replica_groups=mesh['rep'=8,'shard'=4] {'shard'}, use_global_device_ids=true, to_apply=%add | all-reduce | flops 3840 | bytes 15360
  33.0 6.2 %all_gather.37 = bf16[384,384]{1,0:T(8,128)(2,1)S(1)} all-gather(bf16[96,384]{1,0:T(8,128)(2,1)S(1)} %copy-done.13), channel_id=1, replica_groups=mesh['rep'=8,'shard'=4] {'shard'}, dimensions={0}, use_global_device_ids=true | all-gather | bytes 368640 | tf_op jit(solution)/shard_map/all_gather | solution.py:91
  39.2 5.1 %all-gather = bf16[4,1,384]{2,1,0:T(2,128)(2,1)S(1)} all-gather(bf16[1,1,384]{2,1,0:T(2,128)(2,1)S(1)} %reshape.148), channel_id=1, replica_groups=mesh['rep'=8,'shard'=4] {'shard'}, dimensions={0}, use_global_device_ids=true | all-gather | bytes 3840 | tf_op jit(solution)/shard_map/all_gather | solution.py:94
  46.5 6.9 %collective-permute-done.1 = bf16[96,1152]{1,0:T(8,128)(2,1)S(1)} collective-permute-done((bf16[96,1152]{1,0:T(8,128)(2,1)S(1)}, bf16[96,1152]{1,0:T(8,128)(2,1)S(1)}, u32[]{:S(2)}, u32[]{:S(2)}) %collective-permute-start.1) | collective-permute-done | bytes 221216 | tf_op jit(solution)/shard_map/ppermute | solution.py:16
  61.4 4.2 fusion.98
  68.8 2.2 copy.78
  72.7 2.6 copy.80
  76.7 18.9 %while.26 = (s32[]{:T(128)}, bf16[4,2,256,6,64]{2,4,3,1,0:T(8,128)(2,1)}, f32[4,2,6,256,1]{3,2,1,4,0:T(8,128)S(1)}, bf16[4,2,256,6,64]{2,4,3,1,0:T(8,128)(2,1)},...) while((s32[]{:T(128)}, ...), condition=%wide.region_5.6_spmd, body=%wide.region_2.5_spmd.sunk | while | flops 208598016 | bytes 11122769 | solution.py:115
  78.8 2.5 fusion.154
  83.6 2.5 fusion.154
  88.3 2.5 fusion.154
  93.0 2.5 fusion.154
  95.6 4.6 %fusion.117 = (f32[8,256]{1,0:T(8,128)S(1)}, f32[8,256,384]{2,1,0:T(8,128)S(1)}, f32[8,256,384]{2,1,0:T(8,128)}) fusion(f32[384]{0:T(512)S(1)} %copy-done.24, f32[8,384]{1,0:T(8,128)S(1)} %get-tuple-element.197, bf16[8,256,384]{2,1,0:T(8,128)(2,1)S(1)} %copy-done, bf16[8,256,384]{1,2,0:T(8,128)(2,1)} %bitcast.23, bf16[384,384]{1,0:T(8,128)(2,1)S(1)} %all_gather.37), kind=kOutput, calls=%fused_computation.174 | convolution fusion | flops 607909888 | bytes 9754112 | tf_op jit(solution)/shard_map/lsd,de->lse/dot_general | solution.py:36
  103.1 11.0 %multiply_convert_fusion.1 = (bf16[8,256,1536]{2,1,0:T(8,128)(2,1)}, f32[8,256,1536]{2,1,0:T(8,128)}) fusion(f32[1536]{0:T(1024)} %reshape.150, bf16[384,1536]{1,0:T(8,128)(2,1)} %all-gather.7.cloned.1.call-done, f32[8,256,384]{2,1,0:T(8,128)} %copy-done.1, f32[8,384]{1,0:T(8,128)} %get-tuple-element.193, f32[8,384]{1,0:T(8,128)} %get-tuple-element.194, ...), kind=kOutput, calls=%fused_computation.69 | convolution fusion | flops 2451308544 | bytes 23246848 | tf_op jit(solution)/shard_map/lsd,de->lse/dot_general | solution.py:36
  114.2 14.8 %fusion.122 = (bf16[1536]{0:T(1024)(128)(2,1)}, bf16[8,256,1536]{2,1,0:T(8,128)(2,1)S(1)}) fusion(f32[8,256,1536]{2,1,0:T(8,128)} %get-tuple-element.206, f32[1536]{0:T(1024)} %reshape.150, bf16[1536,384]{1,0:T(8,128)(2,1)} %all-gather.9.cloned.1.call-done, bf16[8,256,384]{2,1,0:T(8,128)(2,1)} %param.29, f32[8,384]{1,0:T(8,128)} %get-tuple-element.192), kind=kOutput, calls=%fused_computation.179 | convolution fusion | flops 2487482880 | bytes 21648384 | tf_op jit(solution)/shard_map/lse,de->lsd/dot_general | solution.py:139
  129.0 3.6 fusion.92
  135.9 6.0 %fusion.79 = (bf16[8,384]{1,0:T(8,128)(2,1)}, bf16[8,256,384]{2,1,0:T(8,128)(2,1)}, bf16[8,384]{1,0:T(8,128)(2,1)}, f32[8,256]{1,0:T(8,128)S(1)}, f32[8,256]{1,0:T(8,128)S(1)}, /*index=5*/bf16[8,384]{1,0:T(8,128)(2,1)}) fusion(bf16[8,256,384]{2,1,0:T(8,128)(2,1)S(1)} %copy-done.10, f32[384]{0:T(512)S(1)} %copy-done.35, f32[8,256,384]{2,1,0:T(8,128)S(1)} %copy-done.2, ...), kind=kOutput, calls=%fused_computation.94 | convolution fusion | flops 2428488704 | bytes 16985600 | tf_op jit(solution)/shard_map/lsd,de->lse/dot_general | solution.py:36
  141.9 4.1 fusion.116
  146.0 2.3 convolution_convert_fusion.1
  148.3 3.1 fusion.85
  151.4 2.6 copy.82
  158.0 37.4 %while.27 = (s32[]{:T(128)}, bf16[4,2,256,6,64]{2,4,3,1,0:T(8,128)(2,1)}, bf16[4,2,256,6,64]{2,4,3,1,0:T(8,128)(2,1)}, bf16[4,2,256,6,64]{2,4,3,1,0:T(8,128)(2,1...) while((s32[]{:T(128)}, ...), condition=%wide.region_12.13_spmd, body=%wide.region_10.12_spmd.sunk | while | flops 513733632 | bytes 33916036 | solution.py:154
  159.8 1.9 multiply_reduce_fusion.11
  163.8 2.1 fusion.164
  169.1 1.9 multiply_reduce_fusion.11
  173.1 2.1 fusion.164
  178.4 1.9 multiply_reduce_fusion.11
  182.4 2.1 fusion.164
  191.8 2.2 fusion.164
  195.4 2.8 copy.83
  199.7 2.7 copy.85
  202.6 5.3 %fusion.82 = bf16[384,1152]{1,0:T(8,128)(2,1)} fusion(bf16[8,256,384]{2,1,0:T(8,128)(2,1)S(1)} %copy-done, f32[8,384]{1,0:T(8,128)S(1)} %copy-done.21, f32[8,384]{1,0:T(8,128)S(1)} %get-tuple-element.196, f32[8,256]{1,0:T(8,128)S(1)} %add_rsqrt_fusion.1, f32[8,256]{1,0:T(8,128)S(1)} %broadcast_multiply_fusion.5, bf16[8,256,384]{2,1,0:T(8,128)(2,1)} %copy.85, ...), kind=kOutput, calls=%fused_computation.111 | convolution fusion | flops 1831256064 | bytes 7217152 | tf_op jit(solution)/shard_map/lsd,lse->de/dot_general | solution.py:40
  208.0 7.7 %fusion.83 = bf16[384,1536]{1,0:T(8,128)(2,1)} fusion(bf16[8,256,1536]{2,1,0:T(8,128)(2,1)} %copy-done.39, f32[8,256,384]{2,1,0:T(8,128)} %copy-done.1, f32[8,384]{1,0:T(8,128)S(1)} %copy-done.26, f32[8,384]{1,0:T(8,128)S(1)} %copy-done.19, f32[8,256]{1,0:T(8,128)S(1)} %copy-done.23, f32[8,256]{1,0:T(8,128)S(1)} %broadcast_multiply_fusion.4), kind=kOutput, calls=%fused_computation.112 | convolution fusion | flops 2420441088 | bytes 10657792 | tf_op jit(solution)/shard_map/lsd,lse->de/dot_general | solution.py:40
  215.7 10.8 %all_gather.43 = bf16[384,1152]{1,0:T(8,128)(2,1)} all-gather(bf16[96,1152]{1,0:T(8,128)(2,1)} %param.21), channel_id=1, replica_groups=mesh['rep'=8,'shard'=4] {'shard'}, dimensions={0}, use_global_device_ids=true | all-gather | bytes 1105920 | tf_op jit(solution)/shard_map/all_gather | solution.py:128
  226.6 7.7 %fusion.84 = bf16[1536,384]{1,0:T(8,128)(2,1)} fusion(bf16[8,256,1536]{2,1,0:T(8,128)(2,1)} %get-tuple-element.205, bf16[8,256,384]{2,1,0:T(8,128)(2,1)} %param.29, f32[8,384]{1,0:T(8,128)S(1)} %copy-done.17), kind=kOutput, calls=%fused_computation.113 | convolution fusion | flops 2418868224 | bytes 9056256 | tf_op jit(solution)/shard_map/lsd,lse->de/dot_general | solution.py:40
  234.4 6.2 %fusion.76 = (bf16[8,384]{1,0:T(8,128)(2,1)S(1)}, f32[8,256]{1,0:T(8,128)S(1)}, f32[8,256]{1,0:T(8,128)S(1)}, bf16[8,384]{1,0:T(8,128)(2,1)S(1)}, f32[8,256,384]{2,1,0:T(8,128)S(1)}) fusion(bf16[8,256,384]{2,1,0:T(8,128)(2,1)S(1)} %copy-done, f32[8,256]{1,0:T(8,128)S(1)} %add_rsqrt_fusion.1, f32[8,256]{1,0:T(8,128)S(1)} %broadcast_multiply_fusion.5, ...), kind=kOutput, calls=%fused_computation.91 | convolution fusion | flops 1833949184 | bytes 10379264 | tf_op jit(solution)/shard_map/lse,de->lsd/dot_general | solution.py:168
  240.7 3.1 multiply_reduce_fusion.3
  243.9 1.9 convolution_convert_fusion
  246.0 5.6 %reduce-scatter.8.cloned.1.call-done = bf16[96,1152]{1,0:T(8,128)(2,1)} async-done(((bf16[384,1152]{1,0:T(8,128)(2,1)}), bf16[96,1152]{1,0:T(8,128)(2,1)}) %reduce-scatter.8.cloned.1.call-update) | async-done | bytes 221200 | tf_op jit(solution)/shard_map/reduce_scatter | solution.py:186
  251.5 28.2 %reduce-scatter.12.cloned.1.call-done = bf16[96,1536]{1,0:T(8,128)(2,1)} async-done(((bf16[384,1536]{1,0:T(8,128)(2,1)}), bf16[96,1536]{1,0:T(8,128)(2,1)}) %reduce-scatter.12.cloned.1.call-update) | async-done | bytes 294928 | tf_op jit(solution)/shard_map/reduce_scatter | solution.py:198
  279.7 28.5 %reduce-scatter.14.cloned.1.call-done = bf16[384,384]{1,0:T(8,128)(2,1)} async-done(((bf16[1536,384]{1,0:T(8,128)(2,1)}), bf16[384,384]{1,0:T(8,128)(2,1)}) %reduce-scatter.14.cloned.1.call-update) | async-done | bytes 294928 | tf_op jit(solution)/shard_map/reduce_scatter | solution.py:204
  308.2 32.0 %reduce-scatter.6.cloned.1.call-done = bf16[96,2304]{1,0:T(8,128)(2,1)} async-done(((bf16[384,2304]{1,0:T(8,128)(2,1)}), bf16[96,2304]{1,0:T(8,128)(2,1)}) %reduce-scatter.6.cloned.1.call-update) | async-done | bytes 442384 | tf_op jit(solution)/shard_map/reduce_scatter | solution.py:180
  342.9 2.2 fusion.115
  345.2 10.5 %all-reduce.11 = (bf16[2304]{0:T(1024)(128)(2,1)S(1)}, bf16[768]{0:T(1024)(128)(2,1)S(1)}, bf16[384]{0:T(512)(128)(2,1)S(1)}, bf16[1536]{0:T(1024)(128)(2,1)S(1)}, bf16[384]{0:T(512)(128)(2,1)S(1)}) all-reduce(bf16[2304]{0:T(1024)(128)(2,1)S(1)} %reduce_sum.215, ...), channel_id=3, replica_groups=mesh['rep'=8,'shard'=4] {'shard'}, use_global_device_ids=true, to_apply=%region_24.25.clone | all-reduce | flops 5376 | bytes 21504
  356.1 22.2 %all-reduce.9 = (bf16[576]{0:T(1024)(128)(2,1)S(1)}, bf16[192]{0:T(256)(128)(2,1)S(1)}, bf16[96]{0:T(256)(128)(2,1)S(1)}, bf16[384]{0:T(512)(128)(2,1)S(1)}, bf16[96]{0:T(256)(128)(2,1)S(1)}) all-reduce(bf16[576]{0:T(1024)(128)(2,1)S(1)} %dynamic-slice.5, ...), channel_id=1, replica_groups=mesh['rep'=8,'shard'=4] {'rep'}, use_global_device_ids=true, to_apply=%region_25.26 | all-reduce | flops 1344 | bytes 5376 | tf_op jit(solution)/shard_map/psum | solution.py:213
  382.2 48.0 %all-reduce.15.cloned.1.call-done = (bf16[96,2304]{1,0:T(8,128)(2,1)}, bf16[96,1152]{1,0:T(8,128)(2,1)}, bf16[96,384]{1,0:T(8,128)(2,1)}, bf16[96,1536]{1,0:T(8,128)(2,1)}, bf16[384,384]{1,0:T(8,128)(2,1)}) async-done(((bf16[96,2304]{1,0:T(8,128)(2,1)}, bf16[96,1152]{1,0:T(8,128)(2,1)}, bf16[96,384]{1,0:T(8,128)(2,1)}, bf16[96,1536]{1,0:T(8,128)(2,1)}, bf16[384,384]{1,0:T(8,128)(2,1)}), ...) | async-done | bytes 1327120 | tf_op jit(solution)/shard_map/psum | solution.py:212
  430.2 2.0 convert_element_type.189
  (216 shorter events, 80.0 us)
Async XLA Ops:
  7.2 47.5 %copy-start.9 = (bf16[96,1152]{1,0:T(8,128)(2,1)S(1)}, bf16[96,1152]{1,0:T(8,128)(2,1)}, u32[]{:S(2)}) copy-start(bf16[96,1152]{1,0:T(8,128)(2,1)} %param.21) | copy-start | bytes 663556
  7.2 24.3 %copy-start = (bf16[8,256,384]{2,1,0:T(8,128)(2,1)S(1)}, bf16[8,256,384]{2,1,0:T(8,128)(2,1)}, u32[]{:S(2)}) copy-start(bf16[8,256,384]{2,1,0:T(8,128)(2,1)} %param.17) | copy-start | bytes 4718596
  7.2 25.8 %copy-start.13 = (bf16[96,384]{1,0:T(8,128)(2,1)S(1)}, bf16[96,384]{1,0:T(8,128)(2,1)}, u32[]{:S(2)}) copy-start(bf16[96,384]{1,0:T(8,128)(2,1)} %param.23) | copy-start | bytes 221188
  7.2 31.9 %copy-start.36 = (bf16[384]{0:T(512)(128)(2,1)S(1)}, bf16[384]{0:T(512)(128)(2,1)}, u32[]{:S(2)}) copy-start(bf16[384]{0:T(512)(128)(2,1)} %param.26) | copy-start | bytes 2308
  7.2 51.7 %all-gather.5.cloned.1.call-start = ((), (), s32[]{:S(2)}) async-start(), calls=%async_computation.5 | async-start | bytes 2211840 | tf_op jit(solution)/shard_map/all_gather | solution.py:87
  8.0 95.2 %all-gather.7.cloned.1.call-start = ((), (), s32[]{:S(2)}) async-start(), calls=%async_computation.6 | async-start | bytes 1474560 | tf_op jit(solution)/shard_map/all_gather | solution.py:93
  8.7 105.5 %all-gather.9.cloned.1.call-start = ((), (), s32[]{:S(2)}) async-start(), calls=%async_computation.7 | async-start | bytes 1474560 | tf_op jit(solution)/shard_map/all_gather | solution.py:95
  8.8 36.8 %collective-permute-start = (bf16[96,1152]{1,0:T(8,128)(2,1)}, bf16[96,1152]{1,0:T(8,128)(2,1)S(1)}, u32[]{:S(2)}, u32[]{:S(2)}) collective-permute-start(bf16[96,1152]{1,0:T(8,128)(2,1)} %param.21), channel_id=1, source_target_pairs={{0,1},{1,2},{2,3},{3,0},{4,5},{5,6},{6,7},{7,4},{8,9},{9,10},{10,1... | collective-permute-start | bytes 663560 | tf_op jit(solution)/shard_map/ppermute | solution.py:16
  9.3 46.2 %collective-permute-start.2 = (bf16[96,1152]{1,0:T(8,128)(2,1)}, bf16[96,1152]{1,0:T(8,128)(2,1)S(1)}, u32[]{:S(2)}, u32[]{:S(2)}) collective-permute-start(bf16[96,1152]{1,0:T(8,128)(2,1)} %param.21), channel_id=1, source_target_pairs={{0,3},{1,0},{2,1},{3,2},{4,7},{5,4},{6,5},{7,6},{8,11},{9,8},{10,9... | collective-permute-start | bytes 663560 | tf_op jit(solution)/shard_map/ppermute | solution.py:18
  11.3 234.7 %reduce-scatter.10.cloned.1.call-start = ((), (), s32[]{:S(2)}) async-start(), calls=%async_computation.10 | async-start | bytes 368640 | tf_op jit(solution)/shard_map/reduce_scatter | solution.py:192
  31.5 27.5 %copy-start.14 = (bf16[8,384]{1,0:T(8,128)(2,1)S(1)}, bf16[8,384]{1,0:T(8,128)(2,1)}, u32[]{:S(2)}) copy-start(bf16[8,384]{1,0:T(8,128)(2,1)} %param.18) | copy-start | bytes 18436
  45.5 7.8 %collective-permute-start.1 = (bf16[96,1152]{1,0:T(8,128)(2,1)S(1)}, bf16[96,1152]{1,0:T(8,128)(2,1)S(1)}, u32[]{:S(2)}, u32[]{:S(2)}) collective-permute-start(bf16[96,1152]{1,0:T(8,128)(2,1)S(1)} %collective-permute-done), channel_id=1, source_target_pairs={{0,1},{1,2},{2,3},{3,0},{4,5},{5,6},{6,7},{7,4},{8,9},{9,10},{10,1... | collective-permute-start | bytes 663560 | tf_op jit(solution)/shard_map/ppermute | solution.py:16
  61.4 4.2 copy-start.20
  76.6 18.9 %copy-start.24 = (f32[384]{0:T(512)S(1)}, f32[384]{0:T(512)}, u32[]{:S(2)}) copy-start(f32[384]{0:T(512)} %convert_element_type.177) | copy-start | bytes 4612
  114.2 14.8 %copy-start.37 = (bf16[384,1536]{1,0:T(8,128)(2,1)S(1)}, bf16[384,1536]{1,0:T(8,128)(2,1)}, u32[]{:S(2)}) copy-start(bf16[384,1536]{1,0:T(8,128)(2,1)} %all-gather.7.cloned.1.call-done) | copy-start | bytes 3538948
  129.0 3.7 copy-start.39
  129.0 4.2 copy-start.2
  129.0 4.6 %copy-start.10 = (bf16[8,256,384]{2,1,0:T(8,128)(2,1)S(1)}, bf16[8,256,384]{2,1,0:T(8,128)(2,1)}, u32[]{:S(2)}) copy-start(bf16[8,256,384]{2,1,0:T(8,128)(2,1)} %param.29) | copy-start | bytes 4718596
  129.0 4.6 %copy-start.16 = (f32[8,384]{1,0:T(8,128)S(1)}, f32[8,384]{1,0:T(8,128)}, u32[]{:S(2)}) copy-start(f32[8,384]{1,0:T(8,128)} %get-tuple-element.192) | copy-start | bytes 36868
  129.0 4.6 %copy-start.18 = (f32[8,384]{1,0:T(8,128)S(1)}, f32[8,384]{1,0:T(8,128)}, u32[]{:S(2)}) copy-start(f32[8,384]{1,0:T(8,128)} %get-tuple-element.194) | copy-start | bytes 36868
  129.0 4.6 %copy-start.22 = (f32[8,256]{1,0:T(8,128)S(1)}, f32[8,256]{1,0:T(8,128)}, u32[]{:S(2)}) copy-start(f32[8,256]{1,0:T(8,128)} %add_rsqrt_fusion) | copy-start | bytes 24580
  129.0 4.6 %copy-start.35 = (f32[384]{0:T(512)S(1)}, f32[384]{0:T(512)}, u32[]{:S(2)}) copy-start(f32[384]{0:T(512)} %convert_element_type.181) | copy-start | bytes 4612
  129.0 5.0 %copy-start.38 = (bf16[1536,384]{1,0:T(8,128)(2,1)S(1)}, bf16[1536,384]{1,0:T(8,128)(2,1)}, u32[]{:S(2)}) copy-start(bf16[1536,384]{1,0:T(8,128)(2,1)} %all-gather.9.cloned.1.call-done) | copy-start | bytes 3538948
  129.0 6.8 %copy-start.40 = (bf16[8,256,1536]{2,1,0:T(8,128)(2,1)S(1)}, bf16[8,256,1536]{2,1,0:T(8,128)(2,1)}, u32[]{:S(2)}) copy-start(bf16[8,256,1536]{2,1,0:T(8,128)(2,1)} %get-tuple-element.205) | copy-start | bytes 18874372
  198.1 4.4 copy-start.21
  199.7 2.9 copy-start.8
  202.5 5.5 %copy-start.19 = (f32[8,384]{1,0:T(8,128)S(1)}, f32[8,384]{1,0:T(8,128)}, u32[]{:S(2)}) copy-start(f32[8,384]{1,0:T(8,128)} %get-tuple-element.194) | copy-start | bytes 36868
  202.5 5.5 %copy-start.23 = (f32[8,256]{1,0:T(8,128)S(1)}, f32[8,256]{1,0:T(8,128)}, u32[]{:S(2)}) copy-start(f32[8,256]{1,0:T(8,128)} %add_rsqrt_fusion) | copy-start | bytes 24580
  202.5 5.5 %copy-start.26 = (f32[8,384]{1,0:T(8,128)S(1)}, f32[8,384]{1,0:T(8,128)}, u32[]{:S(2)}) copy-start(f32[8,384]{1,0:T(8,128)} %get-tuple-element.193) | copy-start | bytes 36868
  202.5 49.0 %reduce-scatter.8.cloned.1.call-start = ((), (), s32[]{:S(2)}) async-start(), calls=%async_computation.9 | async-start | bytes 1105920 | tf_op jit(solution)/shard_map/reduce_scatter | solution.py:186
  207.9 18.7 %copy-start.17 = (f32[8,384]{1,0:T(8,128)S(1)}, f32[8,384]{1,0:T(8,128)}, u32[]{:S(2)}) copy-start(f32[8,384]{1,0:T(8,128)} %get-tuple-element.192) | copy-start | bytes 36868
  207.9 71.8 %reduce-scatter.12.cloned.1.call-start = ((), (), s32[]{:S(2)}) async-start(), calls=%async_computation.11 | async-start | bytes 1474560 | tf_op jit(solution)/shard_map/reduce_scatter | solution.py:198
  215.7 92.5 %reduce-scatter.14.cloned.1.call-start = ((), (), s32[]{:S(2)}) async-start(), calls=%async_computation.12 | async-start | bytes 1474560 | tf_op jit(solution)/shard_map/reduce_scatter | solution.py:204
  234.3 6.3 %copy-start.25 = (f32[384]{0:T(512)S(1)}, f32[384]{0:T(512)}, u32[]{:S(2)}) copy-start(f32[384]{0:T(512)} %convert_element_type.177) | copy-start | bytes 4612
  234.3 105.9 %reduce-scatter.6.cloned.1.call-start = ((), (), s32[]{:S(2)}) async-start(), calls=%async_computation.8 | async-start | bytes 2211840 | tf_op jit(solution)/shard_map/reduce_scatter | solution.py:180
  234.4 6.3 %copy-start.4 = (f32[8,256,384]{2,1,0:T(8,128)S(1)}, f32[8,256,384]{2,1,0:T(8,128)}, u32[]{:S(2)}) copy-start(f32[8,256,384]{2,1,0:T(8,128)} %get-tuple-element.204) | copy-start | bytes 9437188
  234.4 6.3 %copy-start.5 = (f32[8,256,384]{2,1,0:T(8,128)S(1)}, f32[8,256,384]{2,1,0:T(8,128)}, u32[]{:S(2)}) copy-start(f32[8,256,384]{2,1,0:T(8,128)} %get-tuple-element.174) | copy-start | bytes 9437188
  240.7 3.2 copy-start.31
  240.7 3.2 copy-start.30
  240.7 3.2 copy-start.29
  240.7 3.2 copy-start.15
  245.9 99.3 %copy-start.32 = (bf16[384]{0:T(512)(128)(2,1)S(1)}, bf16[384]{0:T(512)(128)(2,1)}, u32[]{:S(2)}) copy-start(bf16[384]{0:T(512)(128)(2,1)} %get-tuple-element.172) | copy-start | bytes 2308
  245.9 99.3 %copy-start.33 = (bf16[384]{0:T(512)(128)(2,1)S(1)}, bf16[384]{0:T(512)(128)(2,1)}, u32[]{:S(2)}) copy-start(bf16[384]{0:T(512)(128)(2,1)} %get-tuple-element.191) | copy-start | bytes 2308
  245.9 99.3 %copy-start.34 = (bf16[1536]{0:T(1024)(128)(2,1)S(1)}, bf16[1536]{0:T(1024)(128)(2,1)}, u32[]{:S(2)}) copy-start(bf16[1536]{0:T(1024)(128)(2,1)} %get-tuple-element.208) | copy-start | bytes 9220
  245.9 135.1 %copy-start.6 = (bf16[384,2304]{1,0:T(8,128)(2,1)S(1)}, bf16[384,2304]{1,0:T(8,128)(2,1)}, u32[]{:S(2)}) copy-start(bf16[384,2304]{1,0:T(8,128)(2,1)} %all-gather.5.cloned.1.call-done) | copy-start | bytes 5308420
  245.9 184.3 %all-reduce.15.cloned.1.call-start = ((), (), s32[]{:S(2)}) async-start(), calls=%async_computation.13 | async-start | bytes 2654208 | tf_op jit(solution)/shard_map/psum | solution.py:212
  430.2 5.7 %copy-start.11 = (bf16[96,1152]{1,0:T(8,128)(2,1)S(1)}, bf16[96,1152]{1,0:T(8,128)(2,1)}, u32[]{:S(2)}) copy-start(bf16[96,1152]{1,0:T(8,128)(2,1)} %get-tuple-element.159) | copy-start | bytes 663556
  430.2 6.5 %copy-start.12 = (bf16[96,384]{1,0:T(8,128)(2,1)S(1)}, bf16[96,384]{1,0:T(8,128)(2,1)}, u32[]{:S(2)}) copy-start(bf16[96,384]{1,0:T(8,128)(2,1)} %get-tuple-element.160) | copy-start | bytes 221188
  (8 other events, 14.2 us)
Sparse Core Ops, SparseCore 0:
  9.6 23.7 all-gather.4
  34.9 18.7 all-gather.6
  55.3 17.2 all-gather.8
  202.6 21.8 reduce-scatter.9
  227.6 23.8 reduce-scatter.7
  254.0 25.7 reduce-scatter.11
  282.4 25.6 reduce-scatter.13
  310.8 29.3 reduce-scatter.5
  344.8 85.3 all-reduce.14
